TPU v7x, 32 devices: a whole 2x2x4 slice. The times are simulated.
32 devices in a mesh: beams: 2 (over y), freq: 4 (over z), tm: 2 (over x), sub: 2 (over core).
Axes of the slice: x: 2, y: 2, z: 4, core: 2. Of those that a mesh axis runs over, the one named last changes fastest.
Arguments:
- filterbank: bfloat16 [1024, 4096], P(('beams', 'freq', 'sub'), 'tm'), parts along dimension 0, may hold values from -8 to 8
- delay_shifts: int32 [9, 512], replicated, may hold values from 0 to 256, as said below
- pulse_filters: bfloat16 [6, 256], replicated, may hold values from -0.375 to 0.375
Outputs:
- dedispersed: float32 [1024, 4096], P(('beams', 'freq', 'sub'), 'tm'), parts along dimension 0
There are 2 independent parts, one for each index of `beams`. A program takes and returns all parts, laid end to end along the dimension named above; an argument that names none is the same for every part. Nothing has to cross between parts.
Inputs may be any that keep to these rules, and one draw needn't show every extreme that they name: `delay_shifts`: at level l every shift lies in 0 to 2^l; trial 0 of every subband has shift 0 and its last trial shift 2^l.
All inputs are finite; a program needn't handle non-finite values.
Results may differ from a plain program's by a relative error of at most 0.0035.
Values may be sent and summed in bfloat16 or wider, within the bound.
A program may use at most 64 MiB of HBM per device.

v0:
```python
import functools
import math

import jax
import jax.numpy as jnp
from jax import lax
from jax.experimental import pallas as pl
from jax.experimental.pallas import tpu as pltpu
from jax.sharding import PartitionSpec as P

LANES = 128
PAIRS = 32
WIRE = jnp.bfloat16
EARLY = 2


def round_up(value, step):
    return -(-value // step) * step


def margin_takes(time_len, margin_len, tm_count):
    takes = []
    collected = 0
    for unused in range(min(tm_count - 1, -(-margin_len // time_len))):
        take = min(time_len, round_up(margin_len - collected, LANES))
        takes.append(take)
        collected += take
    return takes


def bit_reverse(value, bit_count):
    result = jnp.int32(0)
    for unused in range(bit_count):
        result = result * 2 + value % 2
        value = value // 2
    return result


def merge_level(shifts, src, dst, level, rows, pitch, local_width, flat_of, run):
    lanes = lax.broadcasted_iota(jnp.int32, (pitch, LANES), 1)
    log_width = local_width.bit_length() - 1
    far = 2**level >= LANES
    pairs = rows // 2
    unroll = min(PAIRS, pairs)
    run = min(run, 2 * unroll)

    def body(step, carry):
        first = step * unroll
        base = first + (first >> log_width) * local_width
        for offset in range(unroll):
            pair = first + offset
            lower = base + offset + (offset >> log_width) * local_width
            upper = lower + local_width
            kept = src[pl.ds(pl.multiple_of(lower * pitch, 8), pitch), :]
            for side in range(2):
                if (2 * offset + side) % run == 0:
                    flat = flat_of(2 * pair)
                    table = shifts.at[level, pl.ds(pl.multiple_of(flat, run), run)]
                out_row = 2 * pair + side
                amount = table[(2 * offset + side) % run]
                start = pl.multiple_of(upper * pitch, 8)
                if far:
                    start = start + (amount >> 7)
                    amount = amount & (LANES - 1)
                here = src[pl.ds(start, pitch), :]
                after = src[pl.ds(start + 1, pitch), :]
                rest = LANES - amount
                turn = rest & (LANES - 1)
                moved = jnp.where(
                    lanes < rest,
                    pltpu.roll(here, turn, 1),
                    pltpu.roll(after, turn, 1),
                )
                dst[pl.ds(pl.multiple_of(out_row * pitch, 8), pitch), :] = kept + moved
        return carry

    lax.fori_loop(0, pairs // unroll, body, 0)


def kernel(
    plan, shifts, filters, bank, out, main_a, main_b, tail_a, tail_b, state_a, state_b, margin,
    main_sent, main_got, tail_sent, tail_got, blocks, taps_mat,
    margin_send, margin_recv, main_send, main_recv, tail_send, tail_recv,
):
    rows, time_len, group_count, sub_count, tm_count, takes, pitch, main_pitch, tail_pitch, main_keep = plan
    level_count, all_channels = shifts.shape
    filter_count, tap_count = filters.shape
    bit_count = group_count.bit_length() - 1
    local_count = level_count - bit_count
    part_rows = rows // group_count
    freq, sub, tm = lax.axis_index("freq"), lax.axis_index("sub"), lax.axis_index("tm")
    position = freq * sub_count + sub
    own_block = bit_reverse(position, bit_count)
    hops = len(takes)

    barrier = pltpu.get_barrier_semaphore()

    def greet(step, carry):
        peer = (position + step) % group_count
        pl.semaphore_signal(
            barrier,
            inc=1,
            device_id={"freq": peer // sub_count, "sub": peer % sub_count},
            device_id_type=pl.DeviceIdType.MESH,
        )
        return carry

    for hop in range(1, hops + 1):
        for way in (-hop, hop):

            @pl.when((tm + way >= 0) & (tm + way < tm_count))
            def _():
                pl.semaphore_signal(
                    barrier, inc=1, device_id={"tm": tm + way}, device_id_type=pl.DeviceIdType.MESH
                )

    lax.fori_loop(1, group_count, greet, 0)

    own_cols = time_len // LANES
    for col in range(own_cols):
        main_a[pl.ds(col, rows, stride=main_pitch), :] = bank[:, pl.ds(col * LANES, LANES)].astype(
            jnp.float32
        )
    for col in range(main_keep, own_cols):
        tail_a[pl.ds(col - main_keep, rows, stride=tail_pitch), :] = bank[
            :, pl.ds(col * LANES, LANES)
        ].astype(jnp.float32)

    def local_level(level, ends, ends_pitch):
        src, dst = ends[level % 2], ends[1 - level % 2]
        merge_level(
            shifts, src, dst, level, rows, ends_pitch, 2**level, lambda row: position * rows + row,
            math.gcd(rows, LANES),
        )

    early = min(EARLY, local_count)
    for level in range(early):
        local_level(level, (main_a, main_b), main_pitch)

    neighbours = jnp.minimum(tm, hops) + jnp.minimum(tm_count - 1 - tm, hops)
    pl.semaphore_wait(barrier, group_count - 1 + neighbours)

    def margin_copy(hop):
        offset = sum(takes[: hop - 1])
        return pltpu.make_async_remote_copy(
            src_ref=bank.at[:, pl.ds(0, takes[hop - 1])],
            dst_ref=margin.at[:, pl.ds(offset, takes[hop - 1])],
            send_sem=margin_send.at[hop - 1],
            recv_sem=margin_recv.at[hop - 1],
            device_id={"tm": tm - hop},
            device_id_type=pl.DeviceIdType.MESH,
        )

    for hop in range(1, hops + 1):

        @pl.when(tm - hop >= 0)
        def _():
            margin_copy(hop).start()

    for level in range(early, local_count):
        local_level(level, (main_a, main_b), main_pitch)

    def packed(source, length, target):
        def pack(step, carry):
            block = bit_reverse((position + step) % group_count, bit_count)
            start = pl.multiple_of(block * length, 8)
            target[step, pl.ds(0, length), :] = source[pl.ds(start, length), :].astype(WIRE)
            return carry

        lax.fori_loop(1, group_count, pack, 0)

    def part_copy(step, slot, source, target, send_sems, recv_sems):
        peer = (position + step) % group_count
        return pltpu.make_async_remote_copy(
            src_ref=source.at[step],
            dst_ref=target.at[slot],
            send_sem=send_sems.at[step],
            recv_sem=recv_sems.at[slot],
            device_id={"freq": peer // sub_count, "sub": peer % sub_count},
            device_id_type=pl.DeviceIdType.MESH,
        )

    main_copy = functools.partial(
        part_copy, source=main_sent, target=main_got, send_sems=main_send, recv_sems=main_recv
    )
    tail_copy = functools.partial(
        part_copy, source=tail_sent, target=tail_got, send_sems=tail_send, recv_sems=tail_recv
    )

    def send_all(make):
        def send(step, carry):
            make(step, position).start()
            return carry

        lax.fori_loop(1, group_count, send, 0)

    main_len, tail_len = part_rows * main_pitch, part_rows * tail_pitch
    main_end, tail_end = (main_a, main_b)[local_count % 2], (tail_a, tail_b)[local_count % 2]
    packed(main_end, main_len, main_sent)
    send_all(main_copy)

    for hop in range(1, hops + 1):
        offset = sum(takes[: hop - 1])
        cols = range(offset // LANES, (offset + takes[hop - 1]) // LANES)

        @pl.when(tm + hop < tm_count)
        def _():
            margin_copy(hop).wait_recv()
            for col in cols:
                tail_a[pl.ds(own_cols - main_keep + col, rows, stride=tail_pitch), :] = margin[
                    :, pl.ds(col * LANES, LANES)
                ].astype(jnp.float32)

        @pl.when(tm + hop >= tm_count)
        def _():
            for col in cols:
                tail_a[pl.ds(own_cols - main_keep + col, rows, stride=tail_pitch), :] = jnp.zeros(
                    (rows, LANES), jnp.float32
                )

    for col in range(own_cols - main_keep + sum(takes) // LANES, tail_pitch):
        tail_a[pl.ds(col, rows, stride=tail_pitch), :] = jnp.zeros((rows, LANES), jnp.float32)

    for level in range(local_count):
        local_level(level, (tail_a, tail_b), tail_pitch)
    packed(tail_end, tail_len, tail_sent)
    send_all(tail_copy)

    span = tap_count + LANES
    all_taps = filters[...].astype(jnp.float32)
    for width in range(filter_count):
        row = jnp.concatenate([all_taps[width : width + 1], jnp.zeros((1, LANES), jnp.float32)], axis=1)
        spread = jnp.broadcast_to(row, (LANES, span))
        turned = pltpu.roll(spread, 0, 1, stride=1, stride_axis=0)
        taps_mat[pl.ds(width * LANES, LANES), :] = turned.astype(jnp.bfloat16)

    def place(group, main_part, tail_part):
        for row in range(part_rows):
            start = pl.multiple_of((group * part_rows + row) * pitch, 8)
            if main_part is not None:
                state_a[pl.ds(start, main_pitch), :] = main_part[row * main_pitch : (row + 1) * main_pitch]
            if tail_part is not None:
                state_a[pl.ds(start + main_keep, tail_pitch), :] = tail_part[
                    row * tail_pitch : (row + 1) * tail_pitch
                ]

    place(
        position,
        main_end[pl.ds(pl.multiple_of(own_block * main_len, 8), main_len), :],
        tail_end[pl.ds(pl.multiple_of(own_block * tail_len, 8), tail_len), :],
    )

    def take_main(step, carry):
        sender = (position + group_count - step) % group_count
        main_copy(step, sender).wait_recv()
        place(sender, main_got[sender, pl.ds(0, main_len), :].astype(jnp.float32), None)
        return carry

    def take_tail(step, carry):
        sender = (position + group_count - step) % group_count
        tail_copy(step, sender).wait_recv()
        place(sender, None, tail_got[sender, pl.ds(0, tail_len), :].astype(jnp.float32))
        return carry

    lax.fori_loop(1, group_count, take_main, 0)
    lax.fori_loop(1, group_count, take_tail, 0)
    src, dst = state_a, state_b

    for section in range(bit_count):
        level = local_count + section
        local_width = part_rows * 2**section
        log_band = local_width.bit_length()
        merge_level(
            shifts, src, dst, level, rows, pitch, local_width,
            lambda row: (row >> log_band) * 2 ** (level + 1)
            + own_block * (2 * local_width)
            + (row & (2 * local_width - 1)),
            2 * local_width,
        )
        src, dst = dst, src

    scale = 1.0 / math.sqrt(all_channels)
    reach = own_cols + tap_count // LANES
    for col in range(reach):
        blocks[pl.ds(col * rows, rows), :] = (src[pl.ds(col, rows, stride=pitch), :] * scale).astype(
            jnp.bfloat16
        )

    chunk_cols = 4
    chunk = chunk_cols * rows
    for first in range(0, own_cols, chunk_cols):
        pieces = [
            blocks[pl.ds((first + lag) * rows, chunk), :] for lag in range(tap_count // LANES + 1)
        ]
        response = lax.dot_general(
            jnp.concatenate(pieces, axis=1),
            taps_mat[...],
            (((1,), (1,)), ((), ())),
            preferred_element_type=jnp.float32,
        )
        energies = []
        for width in range(filter_count):
            part = response[:, width * LANES : (width + 1) * LANES]
            energies.append(0.5 * part * part)
        top = functools.reduce(jnp.maximum, energies)
        total = functools.reduce(jnp.add, [jnp.exp(energy - top) for energy in energies])
        result = jnp.log(total) + top
        for col in range(chunk_cols):
            out[:, pl.ds((first + col) * LANES, LANES)] = result[col * rows : (col + 1) * rows]

    for hop in range(1, hops + 1):

        @pl.when(tm - hop >= 0)
        def _():
            margin_copy(hop).wait_send()

    def finish(step, carry):
        main_copy(step, position).wait_send()
        tail_copy(step, position).wait_send()
        return carry

    lax.fori_loop(1, group_count, finish, 0)


def local(filterbank, delay_shifts, pulse_filters):
    rows, time_len = filterbank.shape
    sub_count, tm_count = lax.axis_size("sub"), lax.axis_size("tm")
    group_count = lax.axis_size("freq") * sub_count
    level_count = delay_shifts.shape[0]
    filter_count, tap_count = pulse_filters.shape
    margin_len = 2**level_count - 1 + tap_count
    takes = margin_takes(time_len, margin_len, tm_count)
    pitch = round_up(-(-(time_len + margin_len) // LANES), 8)
    own_cols = time_len // LANES
    local_count = level_count - (group_count.bit_length() - 1)
    main_pitch = round_up(own_cols, 8)
    main_keep = own_cols - -(-(2**local_count - 1) // LANES)
    tail_pitch = round_up(-(-(time_len + margin_len) // LANES) - main_keep, 8)
    pitch = max(pitch, round_up(main_keep + tail_pitch, 8))
    part_rows = rows // group_count
    main_part = round_up(part_rows * main_pitch, 16)
    tail_part = round_up(part_rows * tail_pitch, 16)
    spare = round_up(2**level_count // LANES + 2, 8)
    plan = (
        rows, time_len, group_count, sub_count, tm_count, takes, pitch, main_pitch, tail_pitch, main_keep,
    )
    reach = time_len // LANES + tap_count // LANES
    return pl.pallas_call(
        functools.partial(kernel, plan),
        out_shape=jax.ShapeDtypeStruct((rows, time_len), jnp.float32),
        in_specs=[
            pl.BlockSpec(memory_space=pltpu.SMEM),
            pl.BlockSpec(memory_space=pltpu.VMEM),
            pl.BlockSpec(memory_space=pltpu.VMEM),
        ],
        out_specs=pl.BlockSpec(memory_space=pltpu.VMEM),
        scratch_shapes=[
            pltpu.VMEM((rows * main_pitch + spare, LANES), jnp.float32),
            pltpu.VMEM((rows * main_pitch + spare, LANES), jnp.float32),
            pltpu.VMEM((rows * tail_pitch + spare, LANES), jnp.float32),
            pltpu.VMEM((rows * tail_pitch + spare, LANES), jnp.float32),
            pltpu.VMEM((rows * pitch + spare, LANES), jnp.float32),
            pltpu.VMEM((rows * pitch + spare, LANES), jnp.float32),
            pltpu.VMEM((rows, max(sum(takes), LANES)), jnp.bfloat16),
            pltpu.VMEM((group_count, main_part, LANES), WIRE),
            pltpu.VMEM((group_count, main_part, LANES), WIRE),
            pltpu.VMEM((group_count, tail_part, LANES), WIRE),
            pltpu.VMEM((group_count, tail_part, LANES), WIRE),
            pltpu.VMEM((reach * rows, LANES), jnp.bfloat16),
            pltpu.VMEM((filter_count * LANES, tap_count + LANES), jnp.bfloat16),
            pltpu.SemaphoreType.DMA((max(len(takes), 1),)),
            pltpu.SemaphoreType.DMA((max(len(takes), 1),)),
            pltpu.SemaphoreType.DMA((group_count,)),
            pltpu.SemaphoreType.DMA((group_count,)),
            pltpu.SemaphoreType.DMA((group_count,)),
            pltpu.SemaphoreType.DMA((group_count,)),
        ],
        compiler_params=pltpu.CompilerParams(collective_id=0, has_side_effects=True),
        name="dedisperse",
    )(delay_shifts, pulse_filters, filterbank)


def solution(mesh):
    in_specs = (P(("beams", "freq", "sub"), "tm"), P(), P())
    out_specs = P(("beams", "freq", "sub"), "tm")
    return jax.shard_map(local, mesh=mesh, in_specs=in_specs, out_specs=out_specs, check_vma=False)
```

profile of v0, /device:TPU:0, one launch (start us, length us, event | category | flops | bytes accessed | tf_op | source)
XLA Modules:
  0.0 22.5 jit_solution(14771065082508087430)
XLA Ops:
  0.0 20.7 %dedisperse.1 = f32[64,2048]{1,0:T(8,128)} custom-call(s32[9,512]{1,0:T(8,128)} %shifts.1, bf16[6,256]{1,0:T(8,128)(2,1)} %filters.1, bf16[64,2048]{1,0:T(8,128)(2,1)} %bank.1), custom_call_target="tpu_custom_call" | custom-call | tf_op jit(solution)/shard_map/dedisperse/pallas_call | solution.py:348
  20.7 1.9 %copy.5 = f32[64,2048]{1,0:T(8,128)} copy(f32[64,2048]{1,0:T(8,128)} %dedisperse.1) | data formatting | bytes 1048576
where the time goes:
time: 22.7 us; the launch traced here: 22.5 us
  Pallas kernels  20.7 us (91%)
  local copies, waits for them, and re-layouts  1.87 us (8%)
    pallas_call x1, Pallas kernels, local(): pl.pallas_call(functools.partial(kernel, plan), out_shape=jax.ShapeDtypeS...  20.7 us
    unnamed x1, local copies, waits for them, and re-layouts  1.87 us

commit v1 on v0

--- a/solution.py
+++ b/solution.py
@@ -64,13 +64,8 @@
                     amount = amount & (LANES - 1)
                 here = src[pl.ds(start, pitch), :]
                 after = src[pl.ds(start + 1, pitch), :]
-                rest = LANES - amount
-                turn = rest & (LANES - 1)
-                moved = jnp.where(
-                    lanes < rest,
-                    pltpu.roll(here, turn, 1),
-                    pltpu.roll(after, turn, 1),
-                )
+                turn = (LANES - amount) & (LANES - 1)
+                moved = pltpu.roll(jnp.where(lanes >= amount, here, after), turn, 1)
                 dst[pl.ds(pl.multiple_of(out_row * pitch, 8), pitch), :] = kept + moved
         return carry
 
@@ -78,9 +73,9 @@
 
 
 def kernel(
-    plan, shifts, filters, bank, out, main_a, main_b, tail_a, tail_b, state_a, state_b, margin,
+    plan, shifts_in, filters_in, bank_in, out, shifts, filters, bank, main_a, main_b, tail_a, tail_b, state_a, state_b, margin,
     main_sent, main_got, tail_sent, tail_got, blocks, taps_mat,
-    margin_send, margin_recv, main_send, main_recv, tail_send, tail_recv,
+    margin_send, margin_recv, main_send, main_recv, tail_send, tail_recv, loaded,
 ):
     rows, time_len, group_count, sub_count, tm_count, takes, pitch, main_pitch, tail_pitch, main_keep = plan
     level_count, all_channels = shifts.shape
@@ -115,6 +110,17 @@
                 )
 
     lax.fori_loop(1, group_count, greet, 0)
+
+    loads = [
+        pltpu.make_async_copy(source, target, loaded.at[index])
+        for index, (source, target) in enumerate(
+            ((bank_in, bank), (shifts_in, shifts), (filters_in, filters))
+        )
+    ]
+    for load in loads:
+        load.start()
+    for load in loads:
+        load.wait()
 
     own_cols = time_len // LANES
     for col in range(own_cols):
@@ -347,14 +353,13 @@
     reach = time_len // LANES + tap_count // LANES
     return pl.pallas_call(
         functools.partial(kernel, plan),
-        out_shape=jax.ShapeDtypeStruct((rows, time_len), jnp.float32),
-        in_specs=[
-            pl.BlockSpec(memory_space=pltpu.SMEM),
-            pl.BlockSpec(memory_space=pltpu.VMEM),
-            pl.BlockSpec(memory_space=pltpu.VMEM),
-        ],
+        out_shape=pltpu.VMEM((rows, time_len), jnp.float32),
+        in_specs=[pl.BlockSpec(memory_space=pl.ANY)] * 3,
         out_specs=pl.BlockSpec(memory_space=pltpu.VMEM),
         scratch_shapes=[
+            pltpu.SMEM(delay_shifts.shape, delay_shifts.dtype),
+            pltpu.VMEM(pulse_filters.shape, pulse_filters.dtype),
+            pltpu.VMEM(filterbank.shape, filterbank.dtype),
             pltpu.VMEM((rows * main_pitch + spare, LANES), jnp.float32),
             pltpu.VMEM((rows * main_pitch + spare, LANES), jnp.float32),
             pltpu.VMEM((rows * tail_pitch + spare, LANES), jnp.float32),
@@ -374,6 +379,7 @@
             pltpu.SemaphoreType.DMA((group_count,)),
             pltpu.SemaphoreType.DMA((group_count,)),
             pltpu.SemaphoreType.DMA((group_count,)),
+            pltpu.SemaphoreType.DMA((3,)),
         ],
         compiler_params=pltpu.CompilerParams(collective_id=0, has_side_effects=True),
         name="dedisperse",

time: 22.7 us -> 18.8 us (0.83)
  Pallas kernels: 20.7 us -> 17.9 us
  local copies, waits for them, and re-layouts: 1.87 us -> 0.8 us
    pallas_call x1, Pallas kernels: 20.7 us -> 17.9 us  [local(): pl.pallas_call(functools.partial(kernel, plan), out_shape=pltpu.VMEM((row...]
    unnamed x1, local copies, waits for them, and re-layouts: 1.87 us -> 0.8 us
where the time goes in v1:
time: 18.8 us; the launch traced here: 18.7 us
  Pallas kernels  17.9 us (95%)
  local copies, waits for them, and re-layouts  0.8 us (4%)
    pallas_call x1, Pallas kernels, local(): pl.pallas_call(functools.partial(kernel, plan), out_shape=pltpu.VMEM((row...  17.9 us
    unnamed x1, local copies, waits for them, and re-layouts  0.8 us

profile of v1, /device:TPU:0, one launch (start us, length us, event | category | flops | bytes accessed | tf_op | source)
XLA Modules:
  0.0 18.7 jit_solution(1816768877800621038)
XLA Ops:
  0.0 17.9 %dedisperse.1 = f32[64,2048]{1,0:T(8,128)S(1)} custom-call(s32[9,512]{1,0:T(8,128)} %shifts_in.1, bf16[6,256]{1,0:T(8,128)(2,1)} %filters_in.1, bf16[64,2048]{1,0:T(8,128)(2,1)} %bank_in.1), custom_call_target="tpu_custom_call" | custom-call | tf_op jit(solution)/shard_map/dedisperse/pallas_call | solution.py:354
  17.9 0.8 %copy.5 = f32[64,2048]{1,0:T(8,128)} copy(f32[64,2048]{1,0:T(8,128)S(1)} %dedisperse.1) | data formatting | bytes 1048576

commit v2 on v1

--- a/solution.py
+++ b/solution.py
@@ -328,7 +328,399 @@
     lax.fori_loop(1, group_count, finish, 0)
 
 
+def relay_kernel(
+    plan, shifts_in, filters_in, bank_in, out, shifts, filters, bank, main_a, main_b, tail_a, tail_b,
+    state_a, state_b, margin, first_stage, halo_stage, first_sent, first_got, mid_sent, mid_got,
+    tail_sent, tail_got, halo, taps_mat, margin_send, margin_recv, first_send, first_recv, mid_send,
+    mid_recv, tail_send, tail_recv, halo_send, halo_recv, loaded,
+):
+    rows, time_len, group_count, sub_count, tm_count, own_cols, first_cols, mid_cols, tail_cols, pitch = plan
+    level_count, all_channels = shifts.shape
+    filter_count, tap_count = filters.shape
+    bit_count = group_count.bit_length() - 1
+    local_count = level_count - bit_count
+    part_rows = rows // group_count
+    freq, sub, tm = lax.axis_index("freq"), lax.axis_index("sub"), lax.axis_index("tm")
+    position = freq * sub_count + sub
+    own_block = bit_reverse(position, bit_count)
+    has_next, has_last = tm + 1 < tm_count, tm > 0
+
+    loads = [
+        pltpu.make_async_copy(source, target, loaded.at[index])
+        for index, (source, target) in enumerate(
+            ((bank_in, bank), (shifts_in, shifts), (filters_in, filters))
+        )
+    ]
+    for load in loads:
+        load.start()
+
+    barrier = pltpu.get_barrier_semaphore()
+
+    def greet(step, carry):
+        peer = (position + step) % group_count
+        pl.semaphore_signal(
+            barrier,
+            inc=1,
+            device_id={"freq": peer // sub_count, "sub": peer % sub_count},
+            device_id_type=pl.DeviceIdType.MESH,
+        )
+        return carry
+
+    lax.fori_loop(1, group_count, greet, 0)
+    for way, present in ((-1, has_last), (1, has_next)):
+
+        @pl.when(present)
+        def _():
+            pl.semaphore_signal(
+                barrier, inc=1, device_id={"tm": tm + way}, device_id_type=pl.DeviceIdType.MESH
+            )
+
+    for load in loads:
+        load.wait()
+
+    for col in range(own_cols):
+        main_a[pl.ds(col, rows, stride=own_cols), :] = bank[:, pl.ds(col * LANES, LANES)].astype(
+            jnp.float32
+        )
+
+    def local_levels(ends, ends_pitch):
+        for level in range(local_count):
+            merge_level(
+                shifts, ends[level % 2], ends[1 - level % 2], level, rows, ends_pitch, 2**level,
+                lambda row: position * rows + row, math.gcd(rows, LANES),
+            )
+        return ends[local_count % 2]
+
+    main_end = local_levels((main_a, main_b), own_cols)
+
+    for row in range(rows):
+        first_stage[pl.ds(row * first_cols, 8), :] = main_end[pl.ds(row * own_cols, 8), :]
+    for block in range(group_count):
+        length = part_rows * first_cols
+        first_sent[block] = first_stage[pl.ds(block * length, length), :].astype(WIRE)
+        mid_sent[block] = jnp.concatenate(
+            [
+                main_end[pl.ds((block * part_rows + row) * own_cols + first_cols, mid_cols), :]
+                for row in range(part_rows)
+            ],
+            axis=0,
+        ).astype(WIRE)
+
+    def part_copy(step, slot, source, target, send_sems, recv_sems):
+        peer = (position + step) % group_count
+        return pltpu.make_async_remote_copy(
+            src_ref=source.at[bit_reverse(peer, bit_count)],
+            dst_ref=target.at[slot],
+            send_sem=send_sems.at[step],
+            recv_sem=recv_sems.at[slot],
+            device_id={"freq": peer // sub_count, "sub": peer % sub_count},
+            device_id_type=pl.DeviceIdType.MESH,
+        )
+
+    first_copy = functools.partial(
+        part_copy, source=first_sent, target=first_got, send_sems=first_send, recv_sems=first_recv
+    )
+    mid_copy = functools.partial(
+        part_copy, source=mid_sent, target=mid_got, send_sems=mid_send, recv_sems=mid_recv
+    )
+    tail_copy = functools.partial(
+        part_copy, source=tail_sent, target=tail_got, send_sems=tail_send, recv_sems=tail_recv
+    )
+
+    def send_all(make):
+        def send(step, carry):
+            make(step, position).start()
+            return carry
+
+        lax.fori_loop(1, group_count, send, 0)
+
+    margin_copy = pltpu.make_async_remote_copy(
+        src_ref=bank.at[:, pl.ds(0, LANES)],
+        dst_ref=margin,
+        send_sem=margin_send.at[0],
+        recv_sem=margin_recv.at[0],
+        device_id={"tm": tm - 1},
+        device_id_type=pl.DeviceIdType.MESH,
+    )
+
+    def halo_copy(slot, source):
+        return pltpu.make_async_remote_copy(
+            src_ref=source,
+            dst_ref=halo.at[slot],
+            send_sem=halo_send.at[slot],
+            recv_sem=halo_recv.at[slot],
+            device_id={"tm": tm - 1},
+            device_id_type=pl.DeviceIdType.MESH,
+        )
+
+    neighbours = jnp.where(has_last, 1, 0) + jnp.where(has_next, 1, 0)
+    pl.semaphore_wait(barrier, group_count - 1 + neighbours)
+
+    @pl.when(has_last)
+    def _():
+        margin_copy.start()
+
+    send_all(first_copy)
+
+    @pl.when(has_last)
+    def _():
+        halo_copy(position, first_sent.at[own_block]).start()
+
+    send_all(mid_copy)
+
+    span = tap_count + LANES
+    all_taps = filters[...].astype(jnp.float32)
+    for width in range(filter_count):
+        row = jnp.concatenate([all_taps[width : width + 1], jnp.zeros((1, LANES), jnp.float32)], axis=1)
+        spread = jnp.broadcast_to(row, (LANES, span))
+        turned = pltpu.roll(spread, 0, 1, stride=1, stride_axis=0)
+        taps_mat[pl.ds(width * LANES, LANES), :] = turned.astype(jnp.bfloat16)
+
+    for row in range(part_rows):
+        start = pl.multiple_of((position * part_rows + row) * pitch, 8)
+        state_a[pl.ds(start, own_cols), :] = main_end[
+            pl.ds(pl.multiple_of((own_block * part_rows + row) * own_cols, 8), own_cols), :
+        ]
+
+    @pl.when(jnp.logical_not(has_next))
+    def _():
+        for row in range(rows):
+            state_a[pl.ds(row * pitch + own_cols, pitch - own_cols), :] = jnp.zeros(
+                (pitch - own_cols, LANES), jnp.float32
+            )
+
+    for col in range(tail_cols):
+        tail_a[pl.ds(col, rows, stride=8), :] = bank[
+            :, pl.ds((own_cols - tail_cols + col) * LANES, LANES)
+        ].astype(jnp.float32)
+
+    @pl.when(has_next)
+    def _():
+        margin_copy.wait_recv()
+        tail_a[pl.ds(tail_cols, rows, stride=8), :] = margin[...].astype(jnp.float32)
+
+    @pl.when(jnp.logical_not(has_next))
+    def _():
+        tail_a[pl.ds(tail_cols, rows, stride=8), :] = jnp.zeros((rows, LANES), jnp.float32)
+
+    tail_end = local_levels((tail_a, tail_b), 8)
+    for block in range(group_count):
+        tail_sent[block] = jnp.concatenate(
+            [tail_end[pl.ds(block * part_rows * 8 + col, part_rows, stride=8), :] for col in range(tail_cols)],
+            axis=0,
+        ).astype(WIRE)
+    send_all(tail_copy)
+
+    def place(group, part, col):
+        for row in range(part_rows):
+            start = (group * part_rows + row) * pitch + col
+            state_a[pl.ds(start, 8), :] = part[row * 8 : (row + 1) * 8]
+
+    def place_tail(group, parts):
+        for col in range(tail_cols):
+            start = group * part_rows * pitch + own_cols - tail_cols + col
+            state_a[pl.ds(start, part_rows, stride=pitch), :] = parts[col]
+
+    def spread_first(stage, group, got, col):
+        length = part_rows * first_cols
+        base = pl.multiple_of(group * (length + 8), 8)
+        stage[pl.ds(base, length), :] = got.astype(jnp.float32)
+        for row in range(part_rows):
+            start = (group * part_rows + row) * pitch + col
+            state_a[pl.ds(start, 8), :] = stage[pl.ds(base + row * first_cols, 8), :]
+
+    place_tail(
+        position,
+        [
+            tail_end[pl.ds(own_block * part_rows * 8 + col, part_rows, stride=8), :]
+            for col in range(tail_cols)
+        ],
+    )
+
+    def take_first(step, carry):
+        sender = (position + group_count - step) % group_count
+        first_copy(step, sender).wait_recv()
+
+        @pl.when(has_last)
+        def _():
+            halo_copy(sender, first_got.at[sender]).start()
+
+        spread_first(halo_stage, sender, first_got[sender], 0)
+        return carry
+
+    def take_mid(step, carry):
+        sender = (position + group_count - step) % group_count
+        mid_copy(step, sender).wait_recv()
+        place(sender, mid_got[sender].astype(jnp.float32), first_cols)
+        return carry
+
+    def take_tail(step, carry):
+        sender = (position + group_count - step) % group_count
+        tail_copy(step, sender).wait_recv()
+        part = tail_got[sender].astype(jnp.float32)
+        place_tail(sender, [part[col * part_rows : (col + 1) * part_rows] for col in range(tail_cols)])
+        return carry
+
+    def take_halo(step, carry):
+        sender = (position + group_count - step) % group_count
+        halo_copy(sender, first_got.at[sender]).wait_recv()
+        spread_first(halo_stage, sender, halo[sender], own_cols)
+        return carry
+
+    lax.fori_loop(1, group_count, take_first, 0)
+    lax.fori_loop(1, group_count, take_mid, 0)
+    lax.fori_loop(1, group_count, take_tail, 0)
+
+    @pl.when(has_next)
+    def _():
+        lax.fori_loop(0, group_count, take_halo, 0)
+
+    src, dst = state_a, state_b
+    for section in range(bit_count):
+        level = local_count + section
+        local_width = part_rows * 2**section
+        log_band = local_width.bit_length()
+        merge_level(
+            shifts, src, dst, level, rows, pitch, local_width,
+            lambda row: (row >> log_band) * 2 ** (level + 1)
+            + own_block * (2 * local_width)
+            + (row & (2 * local_width - 1)),
+            2 * local_width,
+        )
+        src, dst = dst, src
+
+    scale = 1.0 / math.sqrt(all_channels)
+    some = math.gcd(rows, 16)
+    for first in range(0, rows, some):
+        pieces = [
+            jnp.concatenate(
+                [
+                    (src[pl.ds(row * pitch + lag, own_cols), :] * scale).astype(jnp.bfloat16)
+                    for row in range(first, first + some)
+                ],
+                axis=0,
+            )
+            for lag in range(tap_count // LANES + 1)
+        ]
+        result = log_sum(pieces, taps_mat, filter_count)
+        for index in range(some):
+            row = first + index
+            out[pl.ds(row // 8 * 8 * own_cols + row % 8, own_cols, stride=8), :] = result[
+                index * own_cols : (index + 1) * own_cols
+            ]
+
+    @pl.when(has_last)
+    def _():
+        margin_copy.wait_send()
+
+        def finish_halo(slot, carry):
+            halo_copy(slot, first_got.at[slot]).wait_send()
+            return carry
+
+        lax.fori_loop(0, group_count, finish_halo, 0)
+
+    def finish(step, carry):
+        first_copy(step, position).wait_send()
+        mid_copy(step, position).wait_send()
+        tail_copy(step, position).wait_send()
+        return carry
+
+    lax.fori_loop(1, group_count, finish, 0)
+
+
+def relay_plan(filterbank, delay_shifts, pulse_filters):
+    rows, time_len = filterbank.shape
+    sub_count, tm_count = lax.axis_size("sub"), lax.axis_size("tm")
+    group_count = lax.axis_size("freq") * sub_count
+    level_count = delay_shifts.shape[0]
+    tap_count = pulse_filters.shape[1]
+    local_count = level_count - (group_count.bit_length() - 1)
+    own_cols = time_len // LANES
+    tail_cols = 2
+    first_cols = -(-(2**level_count - 2**local_count + tap_count - 1) // LANES)
+    mid_cols = own_cols - first_cols - tail_cols
+    pitch = own_cols + 8
+    part_rows = rows // group_count
+    fits = (
+        part_rows % 8 == 0
+        and own_cols % 8 == 0
+        and 2**local_count <= LANES
+        and first_cols <= 8
+        and mid_cols == 8
+        and tap_count % LANES == 0
+        and part_rows * first_cols % 16 == 0
+        and 2**level_count // LANES + 2 <= 8
+    )
+    plan = (
+        rows, time_len, group_count, sub_count, tm_count, own_cols, first_cols, mid_cols, tail_cols, pitch,
+    )
+    return plan if fits else None
+
+
+def relayed(plan, filterbank, delay_shifts, pulse_filters):
+    rows, time_len, group_count, sub_count, tm_count, own_cols, first_cols, mid_cols, tail_cols, pitch = plan
+    filter_count, tap_count = pulse_filters.shape
+    part_rows = rows // group_count
+    first_len, mid_len, tail_len = part_rows * first_cols, part_rows * mid_cols, part_rows * tail_cols
+    spare = 8
+    flat = pl.pallas_call(
+        functools.partial(relay_kernel, plan),
+        out_shape=pltpu.VMEM((rows * own_cols, LANES), jnp.float32),
+        in_specs=[pl.BlockSpec(memory_space=pl.ANY)] * 3,
+        out_specs=pl.BlockSpec(memory_space=pltpu.VMEM),
+        scratch_shapes=[
+            pltpu.SMEM(delay_shifts.shape, delay_shifts.dtype),
+            pltpu.VMEM(pulse_filters.shape, pulse_filters.dtype),
+            pltpu.VMEM(filterbank.shape, filterbank.dtype),
+            pltpu.VMEM((rows * own_cols + spare, LANES), jnp.float32),
+            pltpu.VMEM((rows * own_cols + spare, LANES), jnp.float32),
+            pltpu.VMEM((rows * 8 + spare, LANES), jnp.float32),
+            pltpu.VMEM((rows * 8 + spare, LANES), jnp.float32),
+            pltpu.VMEM((rows * pitch + spare, LANES), jnp.float32),
+            pltpu.VMEM((rows * pitch + spare, LANES), jnp.float32),
+            pltpu.VMEM((rows, LANES), jnp.bfloat16),
+            pltpu.VMEM((rows * first_cols + spare, LANES), jnp.float32),
+            pltpu.VMEM((group_count * (first_len + 8), LANES), jnp.float32),
+            pltpu.VMEM((group_count, first_len, LANES), WIRE),
+            pltpu.VMEM((group_count, first_len, LANES), WIRE),
+            pltpu.VMEM((group_count, mid_len, LANES), WIRE),
+            pltpu.VMEM((group_count, mid_len, LANES), WIRE),
+            pltpu.VMEM((group_count, tail_len, LANES), WIRE),
+            pltpu.VMEM((group_count, tail_len, LANES), WIRE),
+            pltpu.VMEM((group_count, first_len, LANES), WIRE),
+            pltpu.VMEM((filter_count * LANES, tap_count + LANES), jnp.bfloat16),
+            pltpu.SemaphoreType.DMA((1,)),
+            pltpu.SemaphoreType.DMA((1,)),
+        ]
+        + [pltpu.SemaphoreType.DMA((group_count,)) for unused in range(8)]
+        + [pltpu.SemaphoreType.DMA((3,))],
+        compiler_params=pltpu.CompilerParams(collective_id=0, has_side_effects=True),
+        name="dedisperse",
+    )(delay_shifts, pulse_filters, filterbank)
+    tiled = flat.reshape(rows // 8, own_cols, 8, LANES)
+    return tiled.transpose(0, 2, 1, 3).reshape(rows, time_len)
+
+
+def log_sum(pieces, taps_mat, filter_count):
+    response = lax.dot_general(
+        jnp.concatenate(pieces, axis=1),
+        taps_mat[...],
+        (((1,), (1,)), ((), ())),
+        preferred_element_type=jnp.float32,
+    )
+    energies = []
+    for width in range(filter_count):
+        part = response[:, width * LANES : (width + 1) * LANES]
+        energies.append(0.5 * part * part)
+    top = functools.reduce(jnp.maximum, energies)
+    total = functools.reduce(jnp.add, [jnp.exp(energy - top) for energy in energies])
+    return jnp.log(total) + top
+
+
 def local(filterbank, delay_shifts, pulse_filters):
+    plan = relay_plan(filterbank, delay_shifts, pulse_filters)
+    if plan is not None:
+        return relayed(plan, filterbank, delay_shifts, pulse_filters)
     rows, time_len = filterbank.shape
     sub_count, tm_count = lax.axis_size("sub"), lax.axis_size("tm")
     group_count = lax.axis_size("freq") * sub_count

time: 18.8 us -> 17.1 us (0.910)
  Pallas kernels: 17.9 us -> 16.1 us
    pallas_call x1, Pallas kernels: 17.9 us -> 16.1 us  [relayed(): pl.pallas_call(functools.partial(relay_kernel, plan), out_shape=pltpu.VME...]
where the time goes in v2:
time: 17.1 us; the launch traced here: 16.9 us
  Pallas kernels  16.1 us (94%)
  local copies, waits for them, and re-layouts  0.8 us (5%)
    pallas_call x1, Pallas kernels, relayed(): pl.pallas_call(functools.partial(relay_kernel, plan), out_shape=pltpu.VME...  16.1 us
    unnamed x1, local copies, waits for them, and re-layouts  0.8 us

profile of v2, /device:TPU:0, one launch (start us, length us, event | category | flops | bytes accessed | tf_op | source)
XLA Modules:
  0.0 16.9 jit_solution(4386516646502231365)
XLA Ops:
  0.0 16.1 %dedisperse.1 = f32[1024,128]{1,0:T(8,128)S(1)} custom-call(s32[9,512]{1,0:T(8,128)} %shifts_in.1, bf16[6,256]{1,0:T(8,128)(2,1)} %filters_in.1, bf16[64,2048]{1,0:T(8,128)(2,1)} %bank_in.1), custom_call_target="tpu_custom_call" | custom-call | tf_op jit(solution)/shard_map/dedisperse/pallas_call | solution.py:666
  16.1 0.8 %copy.5 = f32[64,2048]{1,0:T(8,128)} copy(f32[64,2048]{1,0:T(8,128)S(1)} %bitcast.5) | data formatting | bytes 1048576

commit v3 on v2

--- a/solution.py
+++ b/solution.py
@@ -36,10 +36,11 @@
     return result
 
 
-def merge_level(shifts, src, dst, level, rows, pitch, local_width, flat_of, run):
+def merge_level(shifts, src, dst, level, rows, pitch, local_width, flat_of, run, closed=False):
     lanes = lax.broadcasted_iota(jnp.int32, (pitch, LANES), 1)
     log_width = local_width.bit_length() - 1
     far = 2**level >= LANES
+    inside = lax.broadcasted_iota(jnp.int32, (pitch, LANES), 0) < pitch - 1
     pairs = rows // 2
     unroll = min(PAIRS, pairs)
     run = min(run, 2 * unroll)
@@ -64,6 +65,8 @@
                     amount = amount & (LANES - 1)
                 here = src[pl.ds(start, pitch), :]
                 after = src[pl.ds(start + 1, pitch), :]
+                if closed:
+                    after = jnp.where(inside, after, 0.0)
                 turn = (LANES - amount) & (LANES - 1)
                 moved = pltpu.roll(jnp.where(lanes >= amount, here, after), turn, 1)
                 dst[pl.ds(pl.multiple_of(out_row * pitch, 8), pitch), :] = kept + moved
@@ -328,13 +331,20 @@
     lax.fori_loop(1, group_count, finish, 0)
 
 
+def nearest(position, step, bit_count):
+    result, unit = jnp.int32(0), 1
+    for unused in range(bit_count):
+        result = result + (position // unit + step // unit) % 2 * unit
+        unit *= 2
+    return result
+
+
 def relay_kernel(
-    plan, shifts_in, filters_in, bank_in, out, shifts, filters, bank, main_a, main_b, tail_a, tail_b,
-    state_a, state_b, margin, first_stage, halo_stage, first_sent, first_got, mid_sent, mid_got,
-    tail_sent, tail_got, halo, taps_mat, margin_send, margin_recv, first_send, first_recv, mid_send,
-    mid_recv, tail_send, tail_recv, halo_send, halo_recv, loaded,
+    plan, shifts_in, filters_in, bank_in, out, shifts, filters, bank, main_a, main_b, spill_a, spill_b,
+    state_a, state_b, first_stage, halo_stage, sent, got, halo, taps_mat, main_send, main_recv,
+    first_send, first_recv, halo_send, halo_recv, loaded,
 ):
-    rows, time_len, group_count, sub_count, tm_count, own_cols, first_cols, mid_cols, tail_cols, pitch = plan
+    rows, time_len, group_count, sub_count, tm_count, own_cols, first_cols, pitch = plan
     level_count, all_channels = shifts.shape
     filter_count, tap_count = filters.shape
     bit_count = group_count.bit_length() - 1
@@ -344,6 +354,12 @@
     position = freq * sub_count + sub
     own_block = bit_reverse(position, bit_count)
     has_next, has_last = tm + 1 < tm_count, tm > 0
+    first_len, main_len = part_rows * first_cols, part_rows * own_cols
+    kept_cols = first_cols - 1
+    edge_cols = own_cols - kept_cols - 8
+    rest_len = round_up(part_rows * (8 + edge_cols), 16)
+    lanes = lax.broadcasted_iota(jnp.int32, (part_rows, LANES), 1)
+    spill_lane = LANES - 2**local_count
 
     loads = [
         pltpu.make_async_copy(source, target, loaded.at[index])
@@ -378,53 +394,33 @@
     for load in loads:
         load.wait()
 
-    for col in range(own_cols):
-        main_a[pl.ds(col, rows, stride=own_cols), :] = bank[:, pl.ds(col * LANES, LANES)].astype(
-            jnp.float32
-        )
-
-    def local_levels(ends, ends_pitch):
+    def local_levels(ends, ends_pitch, closed):
         for level in range(local_count):
             merge_level(
                 shifts, ends[level % 2], ends[1 - level % 2], level, rows, ends_pitch, 2**level,
-                lambda row: position * rows + row, math.gcd(rows, LANES),
+                lambda row: position * rows + row, math.gcd(rows, LANES), closed,
             )
         return ends[local_count % 2]
 
-    main_end = local_levels((main_a, main_b), own_cols)
-
-    for row in range(rows):
-        first_stage[pl.ds(row * first_cols, 8), :] = main_end[pl.ds(row * own_cols, 8), :]
-    for block in range(group_count):
-        length = part_rows * first_cols
-        first_sent[block] = first_stage[pl.ds(block * length, length), :].astype(WIRE)
-        mid_sent[block] = jnp.concatenate(
-            [
-                main_end[pl.ds((block * part_rows + row) * own_cols + first_cols, mid_cols), :]
-                for row in range(part_rows)
-            ],
-            axis=0,
-        ).astype(WIRE)
-
-    def part_copy(step, slot, source, target, send_sems, recv_sems):
+    def part_copy(step, slot, send_sems, recv_sems, start, length):
         peer = (position + step) % group_count
         return pltpu.make_async_remote_copy(
-            src_ref=source.at[bit_reverse(peer, bit_count)],
-            dst_ref=target.at[slot],
+            src_ref=sent.at[bit_reverse(peer, bit_count), pl.ds(start, length)],
+            dst_ref=got.at[slot, pl.ds(start, length)],
             send_sem=send_sems.at[step],
             recv_sem=recv_sems.at[slot],
             device_id={"freq": peer // sub_count, "sub": peer % sub_count},
             device_id_type=pl.DeviceIdType.MESH,
         )
 
+    main_copy = functools.partial(
+        part_copy, send_sems=main_send, recv_sems=main_recv, start=0, length=main_len
+    )
+    rest_copy = functools.partial(
+        part_copy, send_sems=main_send, recv_sems=main_recv, start=0, length=rest_len
+    )
     first_copy = functools.partial(
-        part_copy, source=first_sent, target=first_got, send_sems=first_send, recv_sems=first_recv
-    )
-    mid_copy = functools.partial(
-        part_copy, source=mid_sent, target=mid_got, send_sems=mid_send, recv_sems=mid_recv
-    )
-    tail_copy = functools.partial(
-        part_copy, source=tail_sent, target=tail_got, send_sems=tail_send, recv_sems=tail_recv
+        part_copy, send_sems=first_send, recv_sems=first_recv, start=main_len, length=first_len
     )
 
     def send_all(make):
@@ -433,15 +429,6 @@
             return carry
 
         lax.fori_loop(1, group_count, send, 0)
-
-    margin_copy = pltpu.make_async_remote_copy(
-        src_ref=bank.at[:, pl.ds(0, LANES)],
-        dst_ref=margin,
-        send_sem=margin_send.at[0],
-        recv_sem=margin_recv.at[0],
-        device_id={"tm": tm - 1},
-        device_id_type=pl.DeviceIdType.MESH,
-    )
 
     def halo_copy(slot, source):
         return pltpu.make_async_remote_copy(
@@ -453,20 +440,60 @@
             device_id_type=pl.DeviceIdType.MESH,
         )
 
-    neighbours = jnp.where(has_last, 1, 0) + jnp.where(has_next, 1, 0)
-    pl.semaphore_wait(barrier, group_count - 1 + neighbours)
+    def wait_all():
+        neighbours = jnp.where(has_last, 1, 0) + jnp.where(has_next, 1, 0)
+        pl.semaphore_wait(barrier, group_count - 1 + neighbours)
 
     @pl.when(has_last)
     def _():
-        margin_copy.start()
-
-    send_all(first_copy)
+        spill_a[pl.ds(0, rows, stride=8), :] = jnp.zeros((rows, LANES), jnp.float32)
+        for col in range(7):
+            spill_a[pl.ds(col + 1, rows, stride=8), :] = bank[:, pl.ds(col * LANES, LANES)].astype(
+                jnp.float32
+            )
+        spill_end = local_levels((spill_a, spill_b), 8, False)
+        for row in range(rows):
+            first_stage[pl.ds(row * first_cols, 8), :] = spill_end[pl.ds(row * 8, 8), :]
+        wide = lax.broadcasted_iota(jnp.int32, (rows, LANES), 1)
+        first_stage[pl.ds(0, rows, stride=first_cols), :] = jnp.where(
+            wide < spill_lane,
+            spill_end[pl.ds(first_cols, rows, stride=8), :],
+            spill_end[pl.ds(0, rows, stride=8), :],
+        )
+        for block in range(group_count):
+            sent[block, pl.ds(main_len, first_len), :] = first_stage[
+                pl.ds(block * first_len, first_len), :
+            ].astype(WIRE)
+        wait_all()
+        send_all(first_copy)
+        halo_copy(position, sent.at[own_block, pl.ds(main_len, first_len)]).start()
+
+    for col in range(own_cols):
+        main_a[pl.ds(col, rows, stride=own_cols), :] = bank[:, pl.ds(col * LANES, LANES)].astype(
+            jnp.float32
+        )
+    main_end = local_levels((main_a, main_b), own_cols, True)
+
+    @pl.when(jnp.logical_not(has_last))
+    def _():
+        for block in range(group_count):
+            sent[block, pl.ds(0, main_len), :] = main_end[pl.ds(block * main_len, main_len), :].astype(WIRE)
+        wait_all()
+        send_all(main_copy)
 
     @pl.when(has_last)
     def _():
-        halo_copy(position, first_sent.at[own_block]).start()
-
-    send_all(mid_copy)
+        for block in range(group_count):
+            first = block * part_rows
+            pieces = [
+                main_end[pl.ds((first + row) * own_cols + kept_cols, 8), :] for row in range(part_rows)
+            ]
+            for col in range(own_cols - edge_cols, own_cols):
+                pieces.append(main_end[pl.ds(first * own_cols + col, part_rows, stride=own_cols), :])
+            for unused in range((rest_len - part_rows * (8 + edge_cols)) // 8):
+                pieces.append(jnp.zeros((8, LANES), jnp.float32))
+            sent[block, pl.ds(0, rest_len), :] = jnp.concatenate(pieces, axis=0).astype(WIRE)
+        send_all(rest_copy)
 
     span = tap_count + LANES
     all_taps = filters[...].astype(jnp.float32)
@@ -489,87 +516,64 @@
                 (pitch - own_cols, LANES), jnp.float32
             )
 
-    for col in range(tail_cols):
-        tail_a[pl.ds(col, rows, stride=8), :] = bank[
-            :, pl.ds((own_cols - tail_cols + col) * LANES, LANES)
-        ].astype(jnp.float32)
-
-    @pl.when(has_next)
-    def _():
-        margin_copy.wait_recv()
-        tail_a[pl.ds(tail_cols, rows, stride=8), :] = margin[...].astype(jnp.float32)
-
-    @pl.when(jnp.logical_not(has_next))
-    def _():
-        tail_a[pl.ds(tail_cols, rows, stride=8), :] = jnp.zeros((rows, LANES), jnp.float32)
-
-    tail_end = local_levels((tail_a, tail_b), 8)
-    for block in range(group_count):
-        tail_sent[block] = jnp.concatenate(
-            [tail_end[pl.ds(block * part_rows * 8 + col, part_rows, stride=8), :] for col in range(tail_cols)],
-            axis=0,
-        ).astype(WIRE)
-    send_all(tail_copy)
-
-    def place(group, part, col):
+    def spread(group, part, col):
+        base = pl.multiple_of(group * (first_len + 8), 8)
+        halo_stage[pl.ds(base, first_len), :] = part.astype(jnp.float32)
         for row in range(part_rows):
             start = (group * part_rows + row) * pitch + col
+            state_a[pl.ds(start, 8), :] = halo_stage[pl.ds(base + row * first_cols + 1, 8), :]
+        return halo_stage[pl.ds(base, part_rows, stride=first_cols), :]
+
+    def forwarded(sender):
+        return halo_copy(sender, got.at[sender, pl.ds(main_len, first_len)])
+
+    def take_first(step, carry):
+        sender = nearest(position, step, bit_count)
+        first_copy(step, sender).wait_recv()
+        forwarded(sender).start()
+        spread(sender, got[sender, pl.ds(main_len, first_len), :], 0)
+        return carry
+
+    def take_rest(step, carry):
+        sender = nearest(position, step, bit_count)
+        rest_copy(step, sender).wait_recv()
+        part = got[sender, pl.ds(0, rest_len), :].astype(jnp.float32)
+        for row in range(part_rows):
+            start = (sender * part_rows + row) * pitch + kept_cols
             state_a[pl.ds(start, 8), :] = part[row * 8 : (row + 1) * 8]
-
-    def place_tail(group, parts):
-        for col in range(tail_cols):
-            start = group * part_rows * pitch + own_cols - tail_cols + col
-            state_a[pl.ds(start, part_rows, stride=pitch), :] = parts[col]
-
-    def spread_first(stage, group, got, col):
-        length = part_rows * first_cols
-        base = pl.multiple_of(group * (length + 8), 8)
-        stage[pl.ds(base, length), :] = got.astype(jnp.float32)
+        for edge in range(edge_cols):
+            start = sender * part_rows * pitch + own_cols - edge_cols + edge
+            state_a[pl.ds(start, part_rows, stride=pitch), :] = part[
+                part_rows * (8 + edge) : part_rows * (9 + edge)
+            ]
+        return carry
+
+    def take_main(step, carry):
+        sender = nearest(position, step, bit_count)
+        main_copy(step, sender).wait_recv()
+        part = got[sender, pl.ds(0, main_len), :].astype(jnp.float32)
         for row in range(part_rows):
-            start = (group * part_rows + row) * pitch + col
-            state_a[pl.ds(start, 8), :] = stage[pl.ds(base + row * first_cols, 8), :]
-
-    place_tail(
-        position,
-        [
-            tail_end[pl.ds(own_block * part_rows * 8 + col, part_rows, stride=8), :]
-            for col in range(tail_cols)
-        ],
-    )
-
-    def take_first(step, carry):
-        sender = (position + group_count - step) % group_count
-        first_copy(step, sender).wait_recv()
-
-        @pl.when(has_last)
-        def _():
-            halo_copy(sender, first_got.at[sender]).start()
-
-        spread_first(halo_stage, sender, first_got[sender], 0)
-        return carry
-
-    def take_mid(step, carry):
-        sender = (position + group_count - step) % group_count
-        mid_copy(step, sender).wait_recv()
-        place(sender, mid_got[sender].astype(jnp.float32), first_cols)
-        return carry
-
-    def take_tail(step, carry):
-        sender = (position + group_count - step) % group_count
-        tail_copy(step, sender).wait_recv()
-        part = tail_got[sender].astype(jnp.float32)
-        place_tail(sender, [part[col * part_rows : (col + 1) * part_rows] for col in range(tail_cols)])
+            start = pl.multiple_of((sender * part_rows + row) * pitch, 8)
+            state_a[pl.ds(start, own_cols), :] = part[row * own_cols : (row + 1) * own_cols]
         return carry
 
     def take_halo(step, carry):
-        sender = (position + group_count - step) % group_count
-        halo_copy(sender, first_got.at[sender]).wait_recv()
-        spread_first(halo_stage, sender, halo[sender], own_cols)
-        return carry
-
-    lax.fori_loop(1, group_count, take_first, 0)
-    lax.fori_loop(1, group_count, take_mid, 0)
-    lax.fori_loop(1, group_count, take_tail, 0)
+        sender = nearest(position, step, bit_count)
+        forwarded(sender).wait_recv()
+        mixed = spread(sender, halo[sender], own_cols)
+        start = sender * part_rows * pitch + own_cols
+        state_a[pl.ds(start + kept_cols, part_rows, stride=pitch), :] = mixed
+        state_a[pl.ds(start - 1, part_rows, stride=pitch), :] += jnp.where(lanes < spill_lane, 0.0, mixed)
+        return carry
+
+    @pl.when(has_last)
+    def _():
+        lax.fori_loop(1, group_count, take_first, 0)
+        lax.fori_loop(1, group_count, take_rest, 0)
+
+    @pl.when(jnp.logical_not(has_last))
+    def _():
+        lax.fori_loop(1, group_count, take_main, 0)
 
     @pl.when(has_next)
     def _():
@@ -611,21 +615,25 @@
 
     @pl.when(has_last)
     def _():
-        margin_copy.wait_send()
-
         def finish_halo(slot, carry):
-            halo_copy(slot, first_got.at[slot]).wait_send()
+            forwarded(slot).wait_send()
             return carry
 
+        def finish_parts(step, carry):
+            first_copy(step, position).wait_send()
+            rest_copy(step, position).wait_send()
+            return carry
+
         lax.fori_loop(0, group_count, finish_halo, 0)
-
-    def finish(step, carry):
-        first_copy(step, position).wait_send()
-        mid_copy(step, position).wait_send()
-        tail_copy(step, position).wait_send()
-        return carry
-
-    lax.fori_loop(1, group_count, finish, 0)
+        lax.fori_loop(1, group_count, finish_parts, 0)
+
+    @pl.when(jnp.logical_not(has_last))
+    def _():
+        def finish_main(step, carry):
+            main_copy(step, position).wait_send()
+            return carry
+
+        lax.fori_loop(1, group_count, finish_main, 0)
 
 
 def relay_plan(filterbank, delay_shifts, pulse_filters):
@@ -636,32 +644,29 @@
     tap_count = pulse_filters.shape[1]
     local_count = level_count - (group_count.bit_length() - 1)
     own_cols = time_len // LANES
-    tail_cols = 2
-    first_cols = -(-(2**level_count - 2**local_count + tap_count - 1) // LANES)
-    mid_cols = own_cols - first_cols - tail_cols
+    reach = 2**level_count - 2**local_count + tap_count - 1
+    first_cols = -(-reach // LANES)
     pitch = own_cols + 8
     part_rows = rows // group_count
     fits = (
         part_rows % 8 == 0
         and own_cols % 8 == 0
-        and 2**local_count <= LANES
-        and first_cols <= 8
-        and mid_cols == 8
+        and 1 < first_cols < 7
+        and first_cols + 7 <= own_cols
+        and reach - (first_cols - 1) * LANES <= LANES - 2**local_count
         and tap_count % LANES == 0
         and part_rows * first_cols % 16 == 0
         and 2**level_count // LANES + 2 <= 8
     )
-    plan = (
-        rows, time_len, group_count, sub_count, tm_count, own_cols, first_cols, mid_cols, tail_cols, pitch,
-    )
+    plan = (rows, time_len, group_count, sub_count, tm_count, own_cols, first_cols, pitch)
     return plan if fits else None
 
 
 def relayed(plan, filterbank, delay_shifts, pulse_filters):
-    rows, time_len, group_count, sub_count, tm_count, own_cols, first_cols, mid_cols, tail_cols, pitch = plan
+    rows, time_len, group_count, sub_count, tm_count, own_cols, first_cols, pitch = plan
     filter_count, tap_count = pulse_filters.shape
     part_rows = rows // group_count
-    first_len, mid_len, tail_len = part_rows * first_cols, part_rows * mid_cols, part_rows * tail_cols
+    first_len, main_len = part_rows * first_cols, part_rows * own_cols
     spare = 8
     flat = pl.pallas_call(
         functools.partial(relay_kernel, plan),
@@ -678,21 +683,14 @@
             pltpu.VMEM((rows * 8 + spare, LANES), jnp.float32),
             pltpu.VMEM((rows * pitch + spare, LANES), jnp.float32),
             pltpu.VMEM((rows * pitch + spare, LANES), jnp.float32),
-            pltpu.VMEM((rows, LANES), jnp.bfloat16),
             pltpu.VMEM((rows * first_cols + spare, LANES), jnp.float32),
             pltpu.VMEM((group_count * (first_len + 8), LANES), jnp.float32),
-            pltpu.VMEM((group_count, first_len, LANES), WIRE),
-            pltpu.VMEM((group_count, first_len, LANES), WIRE),
-            pltpu.VMEM((group_count, mid_len, LANES), WIRE),
-            pltpu.VMEM((group_count, mid_len, LANES), WIRE),
-            pltpu.VMEM((group_count, tail_len, LANES), WIRE),
-            pltpu.VMEM((group_count, tail_len, LANES), WIRE),
+            pltpu.VMEM((group_count, main_len + first_len, LANES), WIRE),
+            pltpu.VMEM((group_count, main_len + first_len, LANES), WIRE),
             pltpu.VMEM((group_count, first_len, LANES), WIRE),
             pltpu.VMEM((filter_count * LANES, tap_count + LANES), jnp.bfloat16),
-            pltpu.SemaphoreType.DMA((1,)),
-            pltpu.SemaphoreType.DMA((1,)),
         ]
-        + [pltpu.SemaphoreType.DMA((group_count,)) for unused in range(8)]
+        + [pltpu.SemaphoreType.DMA((group_count,)) for unused in range(6)]
         + [pltpu.SemaphoreType.DMA((3,))],
         compiler_params=pltpu.CompilerParams(collective_id=0, has_side_effects=True),
         name="dedisperse",

time: 17.1 us -> 15.5 us (0.906)
  Pallas kernels: 16.1 us -> 14.6 us
    pallas_call x1, Pallas kernels: 16.1 us -> 14.6 us  [relayed(): pl.pallas_call(functools.partial(relay_kernel, plan), out_shape=pltpu.VME...]
where the time goes in v3:
time: 15.5 us; the launch traced here: 15.4 us
  Pallas kernels  14.6 us (94%)
  local copies, waits for them, and re-layouts  0.8 us (5%)
    pallas_call x1, Pallas kernels, relayed(): pl.pallas_call(functools.partial(relay_kernel, plan), out_shape=pltpu.VME...  14.6 us
    unnamed x1, local copies, waits for them, and re-layouts  0.8 us

profile of v3, /device:TPU:0, one launch (start us, length us, event | category | flops | bytes accessed | tf_op | source)
XLA Modules:
  0.0 15.4 jit_solution(422627313043314024)
XLA Ops:
  0.0 14.6 %dedisperse.1 = f32[1024,128]{1,0:T(8,128)S(1)} custom-call(s32[9,512]{1,0:T(8,128)} %shifts_in.1, bf16[6,256]{1,0:T(8,128)(2,1)} %filters_in.1, bf16[64,2048]{1,0:T(8,128)(2,1)} %bank_in.1), custom_call_target="tpu_custom_call" | custom-call | tf_op jit(solution)/shard_map/dedisperse/pallas_call | solution.py:671
  14.6 0.8 %copy.5 = f32[64,2048]{1,0:T(8,128)} copy(f32[64,2048]{1,0:T(8,128)S(1)} %bitcast.5) | data formatting | bytes 1048576

commit v4 on v3

--- a/solution.py
+++ b/solution.py
@@ -36,28 +36,32 @@
     return result
 
 
-def merge_level(shifts, src, dst, level, rows, pitch, local_width, flat_of, run, closed=False):
+def merge_level(
+    shifts, src, dst, level, rows, pitch, local_width, flat_of, run, closed=False, own_trials=False, base_row=None
+):
     lanes = lax.broadcasted_iota(jnp.int32, (pitch, LANES), 1)
     log_width = local_width.bit_length() - 1
     far = 2**level >= LANES
     inside = lax.broadcasted_iota(jnp.int32, (pitch, LANES), 0) < pitch - 1
     pairs = rows // 2
     unroll = min(PAIRS, pairs)
+    own_trials = own_trials and unroll % local_width == 0
+    base_row = 0 if base_row is None else base_row
     run = min(run, 2 * unroll)
 
     def body(step, carry):
         first = step * unroll
-        base = first + (first >> log_width) * local_width
+        base = base_row + first + (first >> log_width) * local_width
         for offset in range(unroll):
             pair = first + offset
             lower = base + offset + (offset >> log_width) * local_width
             upper = lower + local_width
             kept = src[pl.ds(pl.multiple_of(lower * pitch, 8), pitch), :]
+            mixed, turns = [], []
             for side in range(2):
                 if (2 * offset + side) % run == 0:
-                    flat = flat_of(2 * pair)
+                    flat = flat_of(base_row + 2 * pair)
                     table = shifts.at[level, pl.ds(pl.multiple_of(flat, run), run)]
-                out_row = 2 * pair + side
                 amount = table[(2 * offset + side) % run]
                 start = pl.multiple_of(upper * pitch, 8)
                 if far:
@@ -67,12 +71,27 @@
                 after = src[pl.ds(start + 1, pitch), :]
                 if closed:
                     after = jnp.where(inside, after, 0.0)
-                turn = (LANES - amount) & (LANES - 1)
-                moved = pltpu.roll(jnp.where(lanes >= amount, here, after), turn, 1)
-                dst[pl.ds(pl.multiple_of(out_row * pitch, 8), pitch), :] = kept + moved
-        return carry
-
-    lax.fori_loop(0, pairs // unroll, body, 0)
+                turns.append((LANES - amount) & (LANES - 1))
+                still = own_trials and side == 0 and offset % local_width == 0
+                mixed.append(here if still else jnp.where(lanes >= amount, here, after))
+                if still:
+                    turns[-1] = None
+            for piece in range(0, pitch, 8):
+                moved = [
+                    value[piece : piece + 8] if turn is None else pltpu.roll(value[piece : piece + 8], turn, 1)
+                    for value, turn in zip(mixed, turns)
+                ]
+                for side in range(2):
+                    out_row = base_row + 2 * pair + side
+                    dst[pl.ds(pl.multiple_of(out_row * pitch, 8) + piece, 8), :] = (
+                        kept[piece : piece + 8] + moved[side]
+                    )
+        return carry
+
+    if pairs == unroll:
+        body(0, 0)
+    else:
+        lax.fori_loop(0, pairs // unroll, body, 0)
 
 
 def kernel(
@@ -398,12 +417,12 @@
         for level in range(local_count):
             merge_level(
                 shifts, ends[level % 2], ends[1 - level % 2], level, rows, ends_pitch, 2**level,
-                lambda row: position * rows + row, math.gcd(rows, LANES), closed,
+                lambda row: position * rows + row, math.gcd(rows, LANES), closed, True,
             )
         return ends[local_count % 2]
 
     def part_copy(step, slot, send_sems, recv_sems, start, length):
-        peer = (position + step) % group_count
+        peer = step - 1 + jnp.where(step - 1 >= position, 1, 0)
         return pltpu.make_async_remote_copy(
             src_ref=sent.at[bit_reverse(peer, bit_count), pl.ds(start, length)],
             dst_ref=got.at[slot, pl.ds(start, length)],
@@ -706,13 +725,14 @@
         (((1,), (1,)), ((), ())),
         preferred_element_type=jnp.float32,
     )
-    energies = []
+    squares = []
     for width in range(filter_count):
         part = response[:, width * LANES : (width + 1) * LANES]
-        energies.append(0.5 * part * part)
-    top = functools.reduce(jnp.maximum, energies)
-    total = functools.reduce(jnp.add, [jnp.exp(energy - top) for energy in energies])
-    return jnp.log(total) + top
+        squares.append(part * part)
+    top = functools.reduce(jnp.maximum, squares)
+    half = 0.5 / math.log(2.0)
+    total = functools.reduce(jnp.add, [jnp.exp2((square - top) * half) for square in squares])
+    return jnp.log(total) + 0.5 * top
 
 
 def local(filterbank, delay_shifts, pulse_filters):

time: 15.5 us -> 15.4 us (level)
  Pallas kernels: 14.6 us -> 14.4 us
    pallas_call x1, Pallas kernels: 14.6 us -> 14.4 us  [relayed(): pl.pallas_call(functools.partial(relay_kernel, plan), out_shape=pltpu.VME...]
where the time goes in v4:
time: 15.4 us; the launch traced here: 15.2 us
  Pallas kernels  14.4 us (94%)
  local copies, waits for them, and re-layouts  0.8 us (5%)
    pallas_call x1, Pallas kernels, relayed(): pl.pallas_call(functools.partial(relay_kernel, plan), out_shape=pltpu.VME...  14.4 us
    unnamed x1, local copies, waits for them, and re-layouts  0.8 us

profile of v4, /device:TPU:0, one launch (start us, length us, event | category | flops | bytes accessed | tf_op | source)
XLA Modules:
  0.0 15.2 jit_solution(10895105572837940853)
XLA Ops:
  0.0 14.4 %dedisperse.1 = f32[1024,128]{1,0:T(8,128)S(1)} custom-call(s32[9,512]{1,0:T(8,128)} %shifts_in.1, bf16[6,256]{1,0:T(8,128)(2,1)} %filters_in.1, bf16[64,2048]{1,0:T(8,128)(2,1)} %bank_in.1), custom_call_target="tpu_custom_call" | custom-call | tf_op jit(solution)/shard_map/dedisperse/pallas_call | solution.py:690
  14.4 0.8 %copy.5 = f32[64,2048]{1,0:T(8,128)} copy(f32[64,2048]{1,0:T(8,128)S(1)} %bitcast.5) | data formatting | bytes 1048576

commit v5 on v4

--- a/solution.py
+++ b/solution.py
@@ -37,9 +37,11 @@
 
 
 def merge_level(
-    shifts, src, dst, level, rows, pitch, local_width, flat_of, run, closed=False, own_trials=False, base_row=None
+    shifts, src, dst, level, rows, pitch, local_width, flat_of, run, closed=False, own_trials=False, base_row=None,
+    window=None,
 ):
-    lanes = lax.broadcasted_iota(jnp.int32, (pitch, LANES), 1)
+    skip, taken = window or (0, pitch)
+    lanes = lax.broadcasted_iota(jnp.int32, (taken, LANES), 1)
     log_width = local_width.bit_length() - 1
     far = 2**level >= LANES
     inside = lax.broadcasted_iota(jnp.int32, (pitch, LANES), 0) < pitch - 1
@@ -56,19 +58,19 @@
             pair = first + offset
             lower = base + offset + (offset >> log_width) * local_width
             upper = lower + local_width
-            kept = src[pl.ds(pl.multiple_of(lower * pitch, 8), pitch), :]
+            kept = src[pl.ds(pl.multiple_of(lower * pitch, 8) + skip, taken), :]
             mixed, turns = [], []
             for side in range(2):
                 if (2 * offset + side) % run == 0:
                     flat = flat_of(base_row + 2 * pair)
                     table = shifts.at[level, pl.ds(pl.multiple_of(flat, run), run)]
                 amount = table[(2 * offset + side) % run]
-                start = pl.multiple_of(upper * pitch, 8)
+                start = pl.multiple_of(upper * pitch, 8) + skip
                 if far:
                     start = start + (amount >> 7)
                     amount = amount & (LANES - 1)
-                here = src[pl.ds(start, pitch), :]
-                after = src[pl.ds(start + 1, pitch), :]
+                here = src[pl.ds(start, taken), :]
+                after = src[pl.ds(start + 1, taken), :]
                 if closed:
                     after = jnp.where(inside, after, 0.0)
                 turns.append((LANES - amount) & (LANES - 1))
@@ -76,14 +78,14 @@
                 mixed.append(here if still else jnp.where(lanes >= amount, here, after))
                 if still:
                     turns[-1] = None
-            for piece in range(0, pitch, 8):
+            for piece in range(0, taken, 8):
                 moved = [
                     value[piece : piece + 8] if turn is None else pltpu.roll(value[piece : piece + 8], turn, 1)
                     for value, turn in zip(mixed, turns)
                 ]
                 for side in range(2):
                     out_row = base_row + 2 * pair + side
-                    dst[pl.ds(pl.multiple_of(out_row * pitch, 8) + piece, 8), :] = (
+                    dst[pl.ds(pl.multiple_of(out_row * pitch, 8) + skip + piece, 8), :] = (
                         kept[piece : piece + 8] + moved[side]
                     )
         return carry
@@ -359,8 +361,8 @@
 
 
 def relay_kernel(
-    plan, shifts_in, filters_in, bank_in, out, shifts, filters, bank, main_a, main_b, spill_a, spill_b,
-    state_a, state_b, first_stage, halo_stage, sent, got, halo, taps_mat, main_send, main_recv,
+    plan, shifts_in, filters_in, bank_in, out, shifts, near_shifts, filters, bank, main_a, main_b, spill_a, spill_b,
+    state_a, state_b, early_a, early_b, first_stage, halo_stage, sent, got, halo, taps_mat, main_send, main_recv,
     first_send, first_recv, halo_send, halo_recv, loaded,
 ):
     rows, time_len, group_count, sub_count, tm_count, own_cols, first_cols, pitch = plan
@@ -380,13 +382,21 @@
     lanes = lax.broadcasted_iota(jnp.int32, (part_rows, LANES), 1)
     spill_lane = LANES - 2**local_count
 
-    loads = [
+    first_span, rest_span = pl.ds(0, 8 * LANES), pl.ds(8 * LANES, time_len - 8 * LANES)
+    near_start = pl.multiple_of(position * rows // LANES * LANES, LANES)
+    load_near, load_first, load_rest, load_filters, load_shifts = [
         pltpu.make_async_copy(source, target, loaded.at[index])
         for index, (source, target) in enumerate(
-            ((bank_in, bank), (shifts_in, shifts), (filters_in, filters))
+            (
+                (shifts_in.at[:, pl.ds(near_start, LANES)], near_shifts),
+                (bank_in.at[:, first_span], bank.at[:, first_span]),
+                (bank_in.at[:, rest_span], bank.at[:, rest_span]),
+                (filters_in, filters),
+                (shifts_in, shifts),
+            )
         )
     ]
-    for load in loads:
+    for load in (load_near, load_first, load_rest, load_filters, load_shifts):
         load.start()
 
     barrier = pltpu.get_barrier_semaphore()
@@ -410,14 +420,14 @@
                 barrier, inc=1, device_id={"tm": tm + way}, device_id_type=pl.DeviceIdType.MESH
             )
 
-    for load in loads:
-        load.wait()
+    load_near.wait()
+    load_first.wait()
 
     def local_levels(ends, ends_pitch, closed):
         for level in range(local_count):
             merge_level(
-                shifts, ends[level % 2], ends[1 - level % 2], level, rows, ends_pitch, 2**level,
-                lambda row: position * rows + row, math.gcd(rows, LANES), closed, True,
+                near_shifts, ends[level % 2], ends[1 - level % 2], level, rows, ends_pitch, 2**level,
+                lambda row: position * rows % LANES + row, math.gcd(rows, LANES), closed, True,
             )
         return ends[local_count % 2]
 
@@ -487,6 +497,7 @@
         send_all(first_copy)
         halo_copy(position, sent.at[own_block, pl.ds(main_len, first_len)]).start()
 
+    load_rest.wait()
     for col in range(own_cols):
         main_a[pl.ds(col, rows, stride=own_cols), :] = bank[:, pl.ds(col * LANES, LANES)].astype(
             jnp.float32
@@ -514,6 +525,7 @@
             sent[block, pl.ds(0, rest_len), :] = jnp.concatenate(pieces, axis=0).astype(WIRE)
         send_all(rest_copy)
 
+    load_filters.wait()
     span = tap_count + LANES
     all_taps = filters[...].astype(jnp.float32)
     for width in range(filter_count):
@@ -594,43 +606,50 @@
     def _():
         lax.fori_loop(1, group_count, take_main, 0)
 
+    scale = 1.0 / math.sqrt(all_channels)
+    some = math.gcd(rows, 256 // (own_cols - 8))
+
+    def finish_cols(ends, window, first_col, col_count):
+        for section in range(bit_count):
+            level = local_count + section
+            local_width = part_rows * 2**section
+            log_band = local_width.bit_length()
+            merge_level(
+                shifts, ends[section], ends[section + 1], level, rows, pitch, local_width,
+                lambda row: (row >> log_band) * 2 ** (level + 1)
+                + own_block * (2 * local_width)
+                + (row & (2 * local_width - 1)),
+                2 * local_width, window=window,
+            )
+        src = ends[bit_count]
+        for first in range(0, rows, some):
+            pieces = [
+                jnp.concatenate(
+                    [
+                        (src[pl.ds(row * pitch + first_col + lag, col_count), :] * scale).astype(jnp.bfloat16)
+                        for row in range(first, first + some)
+                    ],
+                    axis=0,
+                )
+                for lag in range(tap_count // LANES + 1)
+            ]
+            result = log_sum(pieces, taps_mat, filter_count)
+            for index in range(some):
+                row = first + index
+                out[
+                    pl.ds((row // 8 * own_cols + first_col) * 8 + row % 8, col_count, stride=8), :
+                ] = result[index * col_count : (index + 1) * col_count]
+
+    load_shifts.wait()
+    early = ([early_a, early_b] * bit_count)[:bit_count]
+    finish_cols([state_a] + early, (0, own_cols), 0, own_cols - 8)
+
     @pl.when(has_next)
     def _():
         lax.fori_loop(0, group_count, take_halo, 0)
 
-    src, dst = state_a, state_b
-    for section in range(bit_count):
-        level = local_count + section
-        local_width = part_rows * 2**section
-        log_band = local_width.bit_length()
-        merge_level(
-            shifts, src, dst, level, rows, pitch, local_width,
-            lambda row: (row >> log_band) * 2 ** (level + 1)
-            + own_block * (2 * local_width)
-            + (row & (2 * local_width - 1)),
-            2 * local_width,
-        )
-        src, dst = dst, src
-
-    scale = 1.0 / math.sqrt(all_channels)
-    some = math.gcd(rows, 16)
-    for first in range(0, rows, some):
-        pieces = [
-            jnp.concatenate(
-                [
-                    (src[pl.ds(row * pitch + lag, own_cols), :] * scale).astype(jnp.bfloat16)
-                    for row in range(first, first + some)
-                ],
-                axis=0,
-            )
-            for lag in range(tap_count // LANES + 1)
-        ]
-        result = log_sum(pieces, taps_mat, filter_count)
-        for index in range(some):
-            row = first + index
-            out[pl.ds(row // 8 * 8 * own_cols + row % 8, own_cols, stride=8), :] = result[
-                index * own_cols : (index + 1) * own_cols
-            ]
+    late = ([state_a, state_b] * (bit_count + 1))[: bit_count + 1]
+    finish_cols(late, (own_cols - 8, 16), own_cols - 8, 8)
 
     @pl.when(has_last)
     def _():
@@ -669,6 +688,10 @@
     part_rows = rows // group_count
     fits = (
         part_rows % 8 == 0
+        and LANES % rows == 0
+        and own_cols > 8
+        and own_cols == 16
+        and first_cols <= own_cols - 9
         and own_cols % 8 == 0
         and 1 < first_cols < 7
         and first_cols + 7 <= own_cols
@@ -694,12 +717,15 @@
         out_specs=pl.BlockSpec(memory_space=pltpu.VMEM),
         scratch_shapes=[
             pltpu.SMEM(delay_shifts.shape, delay_shifts.dtype),
+            pltpu.SMEM((delay_shifts.shape[0], LANES), delay_shifts.dtype),
             pltpu.VMEM(pulse_filters.shape, pulse_filters.dtype),
             pltpu.VMEM(filterbank.shape, filterbank.dtype),
             pltpu.VMEM((rows * own_cols + spare, LANES), jnp.float32),
             pltpu.VMEM((rows * own_cols + spare, LANES), jnp.float32),
             pltpu.VMEM((rows * 8 + spare, LANES), jnp.float32),
             pltpu.VMEM((rows * 8 + spare, LANES), jnp.float32),
+            pltpu.VMEM((rows * pitch + spare, LANES), jnp.float32),
+            pltpu.VMEM((rows * pitch + spare, LANES), jnp.float32),
             pltpu.VMEM((rows * pitch + spare, LANES), jnp.float32),
             pltpu.VMEM((rows * pitch + spare, LANES), jnp.float32),
             pltpu.VMEM((rows * first_cols + spare, LANES), jnp.float32),
@@ -710,7 +736,7 @@
             pltpu.VMEM((filter_count * LANES, tap_count + LANES), jnp.bfloat16),
         ]
         + [pltpu.SemaphoreType.DMA((group_count,)) for unused in range(6)]
-        + [pltpu.SemaphoreType.DMA((3,))],
+        + [pltpu.SemaphoreType.DMA((5,))],
         compiler_params=pltpu.CompilerParams(collective_id=0, has_side_effects=True),
         name="dedisperse",
     )(delay_shifts, pulse_filters, filterbank)

time: 15.4 us -> 15.2 us (0.987)
  the two profiles are of different devices: /device:TPU:0 before, /device:TPU:1 now
where the time goes in v5:
time: 15.2 us; the launch traced here: 15 us
  Pallas kernels  14.2 us (93%)
  local copies, waits for them, and re-layouts  0.8 us (5%)
    pallas_call x1, Pallas kernels, relayed(): pl.pallas_call(functools.partial(relay_kernel, plan), out_shape=pltpu.VME...  14.2 us
    unnamed x1, local copies, waits for them, and re-layouts  0.8 us

profile of v5, /device:TPU:1, one launch (start us, length us, event | category | flops | bytes accessed | tf_op | source)
XLA Modules:
  0.0 15.0 jit_solution(11531208174168687252)
XLA Ops:
  0.0 14.2 %dedisperse.1 = f32[1024,128]{1,0:T(8,128)S(1)} custom-call(s32[9,512]{1,0:T(8,128)} %shifts_in.1, bf16[6,256]{1,0:T(8,128)(2,1)} %filters_in.1, bf16[64,2048]{1,0:T(8,128)(2,1)} %bank_in.1), custom_call_target="tpu_custom_call" | custom-call | tf_op jit(solution)/shard_map/dedisperse/pallas_call | solution.py:713
  14.2 0.8 %copy.5 = f32[64,2048]{1,0:T(8,128)} copy(f32[64,2048]{1,0:T(8,128)S(1)} %bitcast.5) | data formatting | bytes 1048576
